TPU v7x, 128 devices: a whole 4x4x4 slice. The times are simulated.
128 devices in a mesh: space: 8 (over z, core), mode: 16 (over y, x).
Axes of the slice: x: 4, y: 4, z: 4, core: 2. Of those that a mesh axis runs over, the one named last changes fastest.
Arguments:
- sqrt_factors: bfloat16 [512, 3, 384, 512], P('mode', None, 'space'), may hold values from -10 to 10
- model_error: bfloat16 [256, 3, 384, 512], P(None, None, ('space', 'mode')), may hold values from -6 to 6
- water_depth: float32 [384, 512], P('space'), may hold values from 0.5 to 2
- sea_mask: int32 [384, 512], P('space'), may hold values 0 or 1
- givens_transform: bfloat16 [768, 512], replicated, may hold values from -0.2 to 1.2
Outputs:
- reduced_modes: bfloat16 [512, 3, 384, 512], P('mode', None, 'space')
- gram_matrix: float32 [768, 768], P(('space', 'mode'))
- inflation: float32 [], replicated
All inputs are finite; a program needn't handle non-finite values. No bound on the sum of `sea_mask` on one device may be relied on, other than what follows from the above.
Results may differ from a plain program's by a relative error of at most 0.0049.
Values may be sent and summed in bfloat16 or wider, within the bound.
A program may use at most 128 MiB of HBM per device.

v0:
```python
import jax
import jax.numpy as jnp
from jax import lax
from jax.sharding import PartitionSpec as P

flux_coef = 0.2
slope_coef = 0.2
turn_coef = 0.1
keep_coef = 0.95


def extended(block, sides, width):
    for axis, dim in sides:
        count = lax.axis_size(axis)
        forward = [(i, i + 1) for i in range(count - 1)]
        backward = [(target, source) for source, target in forward]
        low = lax.ppermute(
            lax.slice_in_dim(block, block.shape[dim] - width, None, axis=dim), axis, forward
        )
        high = lax.ppermute(lax.slice_in_dim(block, 0, width, axis=dim), axis, backward)
        block = jnp.concatenate([low, block, high], axis=dim)
    return block


def column_diff(field):
    widths = [(0, 0)] * (field.ndim - 1) + [(1, 1)]
    padded = jnp.pad(field, widths)
    return padded[..., 2:] - padded[..., :-2]


def advance_local(layered_surfaces, depth_cells, wet_cells):
    flow_east = layered_surfaces[:, 1]
    flow_north = layered_surfaces[:, 2]
    flux = jnp.stack([depth_cells * flow_east, depth_cells * flow_north], axis=1)
    flux_ext = extended(flux, (("space", 2),), 1)
    divergence = column_diff(flux_ext[:, 0, 1:-1]) + (flux_ext[:, 1, 2:] - flux_ext[:, 1, :-2])
    surface_new = wet_cells * (layered_surfaces[:, 0] - flux_coef * divergence)
    surface_ext = extended(surface_new.astype(jnp.bfloat16), (("space", 1),), 1).astype(
        surface_new.dtype
    )
    slope_east = column_diff(surface_new)
    slope_north = surface_ext[:, 2:] - surface_ext[:, :-2]
    east_new = wet_cells * (
        keep_coef * flow_east + turn_coef * flow_north - slope_coef * slope_east
    )
    north_new = wet_cells * (
        keep_coef * flow_north - turn_coef * flow_east - slope_coef * slope_north
    )
    return jnp.stack([surface_new, east_new, north_new], axis=1)


def shards(sqrt_factors, model_error, water_depth, sea_mask, givens_transform):
    wet_cells = sea_mask.astype(jnp.float32)
    layered_surfaces = sqrt_factors.astype(jnp.float32)
    for iteration in range(2):
        layered_surfaces = advance_local(layered_surfaces, water_depth, wet_cells)
    prior_factors = layered_surfaces.astype(jnp.bfloat16)
    rebanded_factors = lax.all_to_all(
        prior_factors, "mode", split_axis=2, concat_axis=0, tiled=True
    )
    factor_tally = rebanded_factors.shape[0]
    prior_latitudes = rebanded_factors.reshape(factor_tally, -1)
    model_fault_part = model_error.reshape(model_error.shape[0], -1)
    inner_sum_fn = (((1,), (1,)), ((), ()))
    pairwise_entries = (((0,), (0,)), ((), ()))
    prior_moments = lax.dot_general(
        prior_latitudes, prior_latitudes, inner_sum_fn, preferred_element_type=jnp.float32
    )
    mixed_moments = lax.dot_general(
        prior_latitudes, model_fault_part, inner_sum_fn, preferred_element_type=jnp.float32
    )
    error_gram = lax.dot_general(
        model_fault_part, model_fault_part, inner_sum_fn, preferred_element_type=jnp.float32
    )
    upper = jnp.concatenate([prior_moments, mixed_moments], 1)
    lower = jnp.concatenate([mixed_moments.T, error_gram], 1)
    gram_local = jnp.concatenate([upper, lower], 0)
    truncated_factors = lax.dot_general(
        givens_transform[:factor_tally],
        prior_latitudes,
        pairwise_entries,
        preferred_element_type=jnp.float32,
    )
    truncated_factors = truncated_factors + lax.dot_general(
        givens_transform[factor_tally:],
        model_fault_part,
        pairwise_entries,
        preferred_element_type=jnp.float32,
    )
    cell_count = 3.0 * sqrt_factors.shape[2] * lax.axis_size("space") * sqrt_factors.shape[3]
    rotation_wide = givens_transform.astype(jnp.float32)
    largest_level = lax.Precision.HIGHEST
    row_span = gram_local.shape[0] // lax.axis_size(("space", "mode"))
    first_latitude = lax.axis_index(("space", "mode")) * row_span
    gram_all = lax.psum(gram_local, ("space", "mode")) / cell_count
    gram_rows = lax.dynamic_slice_in_dim(gram_all, first_latitude, row_span, 0)
    trace_full = jnp.trace(gram_all)
    trace_kept = jnp.sum(jnp.dot(gram_all, rotation_wide, precision=largest_level) * rotation_wide)
    inflation = jnp.sqrt(trace_full / trace_kept)
    scaled_rows = (
        (inflation * truncated_factors).reshape(rebanded_factors.shape).astype(jnp.bfloat16)
    )
    reduced_modes = lax.all_to_all(scaled_rows, "mode", split_axis=0, concat_axis=2, tiled=True)
    return (reduced_modes, gram_rows, inflation)


def solution(mesh):
    in_specs = (
        P("mode", None, "space", None),
        P(None, None, ("space", "mode"), None),
        P("space", None),
        P("space", None),
        P(),
    )
    out_specs = (P("mode", None, "space", None), P(("space", "mode"), None), P())
    return jax.shard_map(shards, mesh=mesh, in_specs=in_specs, out_specs=out_specs, check_vma=False)
```

profile of v0, /device:TPU:2, one launch (start us, length us, event | category | flops | bytes accessed | tf_op | source)
XLA Modules:
  0.0 468.0 jit_solution(3184777287592296135)
XLA Ops:
  7.2 0.0 copy-start.6
  7.2 5.1 %copy_convert_fusion = f32[32,3,48,512]{3,0,2,1:T(8,128)S(1)} fusion(bf16[32,3,48,512]{3,2,1,0:T(8,128)(2,1)} %param.5), kind=kLoop, calls=%fused_computation.4 | loop fusion | flops 2359296 | bytes 14155776 | tf_op jit(solution)/shard_map/convert_element_type | solution.py:54
  12.3 0.0 copy-done.6
  12.3 1.1 slice_multiply_fusion.1
  13.4 1.3 collective-permute-start
  14.7 0.0 copy-start.8
  14.7 3.2 collective-permute-start.1
  17.9 0.6 bitcast_multiply_fusion.2
  18.6 0.0 copy-done.8
  18.6 0.0 collective-permute-done
  18.6 0.3 collective-permute-done.1
  18.9 2.7 fusion.40
  21.6 4.4 collective-permute-start.2
  26.0 1.3 collective-permute-start.3
  27.3 0.0 collective-permute-done.2
  27.3 3.7 collective-permute-done.3
  31.1 0.3 maximum_convert_fusion
  31.3 4.8 %broadcast_multiply_fusion = (f32[32,48,512]{2,0,1:T(8,128)S(1)}, f32[32,48,512]{2,0,1:T(8,128)}, f32[32,1,48,512]{3,0,2,1:T(8,128)S(1)}, f32[32,48,512]{2,0,1:T(8,128)}) fusion(f32[48,512]{1,0:T(8,128)S(1)} %copy-done.6, f32[32,48,512]{2,0,1:T(8,128)S(1)} %get-tuple-element.17, f32[32,3,48,512]{3,0,2,1:T(8,128)S(1)} %copy_convert_fusion, ...), kind=kLoop, calls=%fused_computation.68 | loop fusion | flops 12582912 | bytes 28508160 | tf_op jit(solution)/shard_map/mul | solution.py:34
  36.2 1.3 collective-permute-start.4
  37.5 5.2 %collective-permute-start.5 = (f32[32,2,1,512]{3,0,2,1:T(8,128)S(1)}, f32[32,2,1,512]{3,0,2,1:T(8,128)S(1)}, u32[]{:S(2)}, u32[]{:S(2)}) collective-permute-start(f32[32,2,1,512]{3,0,2,1:T(8,128)S(1)} %get-tuple-element.27), channel_id=1, source_target_pairs={{0,16},{16,32},{32,48},{48,64},{64,80},{80,96},{96,112},{1,17},{17... | collective-permute-start | bytes 393224 | tf_op jit(solution)/shard_map/ppermute | solution.py:17
  42.6 0.0 collective-permute-done.4
  42.6 1.0 collective-permute-done.5
  43.6 2.7 fusion.37
  46.3 0.0 copy-start.2
  46.4 4.9 %collective-permute-start.6 = (bf16[32,1,512]{2,0,1:T(8,128)(2,1)S(1)}, bf16[32,1,512]{2,0,1:T(8,128)(2,1)S(1)}, u32[]{:S(2)}, u32[]{:S(2)}) collective-permute-start(bf16[32,1,512]{2,0,1:T(8,128)(2,1)S(1)} %get-tuple-element.32), channel_id=1, source_target_pairs={{0,16},{16,32},{32,48},{48,64},{64,80},{80,96},{96,112},{1,17},{17... | collective-permute-start | bytes 98312 | tf_op jit(solution)/shard_map/ppermute | solution.py:17
  51.2 1.3 collective-permute-start.7
  52.5 0.0 collective-permute-done.6
  52.5 3.7 collective-permute-done.7
  56.3 0.3 maximum_convert_fusion.1
  56.6 0.0 copy-done.3
  56.6 0.0 copy-done.2
  56.6 2.9 fusion.33
  59.5 2.4 pad_maximum_fusion
  62.0 0.0 copy-start.1
  62.0 7.6 %all-to-all-start = ((bf16[32,3,48,512]{3,0,1,2:T(8,128)(2,1)}), bf16[32,3,48,512]{3,0,1,2:T(8,128)(2,1)}, u32[]{:S(2)}, u32[]{:S(2)}) async-start(bf16[32,3,48,512]{3,0,1,2:T(8,128)(2,1)} %pad_maximum_fusion), calls=%async_computation | async-start | bytes 9437184 | tf_op jit(solution)/shard_map/all_to_all | solution.py:58
  69.6 0.2 all-reduce.6.cloned.1.call-start
  69.8 0.0 copy-done.1
  69.8 2.4 copy.30
  72.3 1.5 convolution_bitcast_fusion
  73.8 62.6 %all-to-all-done = bf16[32,3,48,512]{3,0,1,2:T(8,128)(2,1)} async-done(((bf16[32,3,48,512]{3,0,1,2:T(8,128)(2,1)}), bf16[32,3,48,512]{3,0,1,2:T(8,128)(2,1)}, u32[]{:S(2)}, u32[]{:S(2)}) %all-to-all-start) | async-done | bytes 4718624 | tf_op jit(solution)/shard_map/all_to_all | solution.py:58
  136.4 9.1 %copy.29 = bf16[16,32,3,3,512]{4,3,2,1,0:T(4,128)(2,1)} copy(bf16[16,32,3,3,512]{4,1,2,3,0:T(8,128)(2,1)} %bitcast.15) | data formatting | bytes 9437184 | tf_op jit(solution)/shard_map/all_to_all | solution.py:58
  145.5 13.5 %reshape.23 = bf16[512,4608]{1,0:T(8,128)(2,1)} reshape(bf16[16,32,3,3,512]{4,3,2,1,0:T(4,128)(2,1)} %copy.29) | data formatting | bytes 9437184 | tf_op jit(solution)/shard_map/reshape | solution.py:62
  159.0 7.5 %fusion.45 = f32[512,512]{0,1:T(8,128)} fusion(bf16[512,4608]{1,0:T(8,128)(2,1)} %reshape.23), kind=kOutput, calls=%fused_computation.85 | convolution fusion | flops 2415919104 | bytes 5767168 | tf_op jit(solution)/shard_map/dot_general | solution.py:66
  166.5 0.0 copy-done
  166.5 0.0 copy-done.4
  166.5 1.4 fusion.46
  167.9 0.2 copy.31
  168.1 2.9 maximum_maximum_fusion
  171.0 0.0 all-reduce.6.cloned.1.call-update
  171.1 8.7 %fusion.34 = f32[4608,512]{1,0:T(8,128)} fusion(bf16[512,4608]{1,0:T(8,128)(2,1)} %reshape.23, bf16[768,512]{1,0:T(8,128)(2,1)} %param.9), kind=kOutput, calls=%fused_computation.73 | convolution fusion | flops 2415919104 | bytes 14680064 | tf_op jit(solution)/shard_map/dot_general | solution.py:78
  179.8 148.6 %all-reduce.6.cloned.1.call-done = f32[768,768]{0,1:T(8,128)} async-done(((f32[768,768]{0,1:T(8,128)}), f32[768,768]{0,1:T(8,128)}) %all-reduce.6.cloned.1.call-update) | async-done | bytes 2359312 | tf_op jit(solution)/shard_map/psum | solution.py:95
  328.4 4.1 broadcast_multiply_fusion.1
  332.5 0.0 copy-done.7
  332.5 0.0 copy-done.5
  332.5 2.9 multiply_reduce_fusion
  336.7 7.3 %fusion.1 = bf16[512,4608]{0,1:T(8,128)(2,1)} fusion(f32[4608,512]{1,0:T(8,128)} %fusion.34, bf16[256,4608]{0,1:T(8,128)(2,1)S(1)} %bitcast.83, f32[]{:T(128)} %sqrt.3, bf16[768,512]{1,0:T(8,128)(2,1)S(1)} %copy-done.7), kind=kOutput, calls=%fused_computation.2 | convolution fusion | flops 1215037440 | bytes 16777220 | tf_op jit(solution)/shard_map/dot_general | solution.py:84
  344.0 11.0 %copy.33 = bf16[512,3,3,512]{3,2,1,0:T(4,128)(2,1)} copy(bf16[512,3,3,512]{0,3,2,1:T(8,128)(2,1)} %bitcast.78) | data formatting | bytes 9437184 | tf_op jit(solution)/shard_map/convert_element_type | solution.py:101
  355.0 6.4 %all-to-all-start.1 = ((bf16[512,3,3,512]{3,2,1,0:T(4,128)(2,1)}), bf16[512,3,3,512]{3,2,1,0:T(4,128)(2,1)}, u32[]{:S(2)}, u32[]{:S(2)}) async-start(bf16[512,3,3,512]{3,2,1,0:T(4,128)(2,1)} %copy.33), calls=%async_computation.1 | async-start | bytes 12582912 | tf_op jit(solution)/shard_map/all_to_all | solution.py:103
  361.4 1.3 constant_dynamic-slice_fusion
  362.7 0.8 copy.37
  363.5 87.0 %all-to-all-done.1 = bf16[512,3,3,512]{3,2,1,0:T(4,128)(2,1)} async-done(((bf16[512,3,3,512]{3,2,1,0:T(4,128)(2,1)}), bf16[512,3,3,512]{3,2,1,0:T(4,128)(2,1)}, u32[]{:S(2)}, u32[]{:S(2)}) %all-to-all-start.1) | async-done | bytes 4718624 | tf_op jit(solution)/shard_map/all_to_all | solution.py:103
  450.5 4.0 copy.34
  454.5 0.7 copy.35
  455.2 4.9 %copy.36 = bf16[32,3,48,512]{3,2,1,0:T(8,128)(2,1)} copy(bf16[32,3,48,512]{3,0,2,1:T(8,128)(2,1)S(1)} %bitcast.79) | data formatting | bytes 9437184
  (10 shorter events, 0.1 us)
Async XLA Ops:
  7.2 5.1 %copy-start.6 = (f32[48,512]{1,0:T(8,128)S(1)}, f32[48,512]{1,0:T(8,128)}, u32[]{:S(2)}) copy-start(f32[48,512]{1,0:T(8,128)} %param.7) | copy-start | bytes 294916
  13.4 5.2 %collective-permute-start = (f32[32,2,1,512]{3,0,2,1:T(8,128)S(1)}, f32[32,2,1,512]{3,0,2,1:T(8,128)S(1)}, u32[]{:S(2)}, u32[]{:S(2)}) collective-permute-start(f32[32,2,1,512]{3,0,2,1:T(8,128)S(1)} %get-tuple-element.28), channel_id=1, source_target_pairs={{16,0},{32,16},{48,32},{64,48},{80,64},{96,80},{112,96},{17,1},{33... | collective-permute-start | bytes 393224 | tf_op jit(solution)/shard_map/ppermute | solution.py:20
  14.7 3.8 copy-start.8
  14.7 4.1 collective-permute-start.1
  21.6 5.7 %collective-permute-start.2 = (bf16[32,1,512]{2,0,1:T(8,128)(2,1)S(1)}, bf16[32,1,512]{2,0,1:T(8,128)(2,1)S(1)}, u32[]{:S(2)}, u32[]{:S(2)}) collective-permute-start(bf16[32,1,512]{2,0,1:T(8,128)(2,1)S(1)} %get-tuple-element.34), channel_id=1, source_target_pairs={{0,16},{16,32},{32,48},{48,64},{64,80},{80,96},{96,112},{1,17},{17... | collective-permute-start | bytes 98312 | tf_op jit(solution)/shard_map/ppermute | solution.py:17
  26.0 5.1 %collective-permute-start.3 = (bf16[32,1,512]{2,0,1:T(8,128)(2,1)S(1)}, bf16[32,1,512]{2,0,1:T(8,128)(2,1)S(1)}, u32[]{:S(2)}, u32[]{:S(2)}) collective-permute-start(bf16[32,1,512]{2,0,1:T(8,128)(2,1)S(1)} %get-tuple-element.35), channel_id=1, source_target_pairs={{16,0},{32,16},{48,32},{64,48},{80,64},{96,80},{112,96},{17,1},{33... | collective-permute-start | bytes 98312 | tf_op jit(solution)/shard_map/ppermute | solution.py:20
  36.2 6.5 %collective-permute-start.4 = (f32[32,2,1,512]{3,0,2,1:T(8,128)S(1)}, f32[32,2,1,512]{3,0,2,1:T(8,128)S(1)}, u32[]{:S(2)}, u32[]{:S(2)}) collective-permute-start(f32[32,2,1,512]{3,0,2,1:T(8,128)S(1)} %get-tuple-element.26), channel_id=1, source_target_pairs={{16,0},{32,16},{48,32},{64,48},{80,64},{96,80},{112,96},{17,1},{33... | collective-permute-start | bytes 393224 | tf_op jit(solution)/shard_map/ppermute | solution.py:20
  37.5 6.1 %collective-permute-start.5 = (f32[32,2,1,512]{3,0,2,1:T(8,128)S(1)}, f32[32,2,1,512]{3,0,2,1:T(8,128)S(1)}, u32[]{:S(2)}, u32[]{:S(2)}) collective-permute-start(f32[32,2,1,512]{3,0,2,1:T(8,128)S(1)} %get-tuple-element.27), channel_id=1, source_target_pairs={{0,16},{16,32},{32,48},{48,64},{64,80},{80,96},{96,112},{1,17},{17... | collective-permute-start | bytes 393224 | tf_op jit(solution)/shard_map/ppermute | solution.py:17
  43.6 13.0 %copy-start.3 = (f32[32,48,512]{2,0,1:T(8,128)S(1)}, f32[32,48,512]{2,0,1:T(8,128)}, u32[]{:S(2)}) copy-start(f32[32,48,512]{2,0,1:T(8,128)} %get-tuple-element.21) | copy-start | bytes 9437188
  46.3 10.2 %copy-start.2 = (f32[32,48,512]{2,0,1:T(8,128)S(1)}, f32[32,48,512]{2,0,1:T(8,128)}, u32[]{:S(2)}) copy-start(f32[32,48,512]{2,0,1:T(8,128)} %get-tuple-element.19) | copy-start | bytes 9437188
  46.4 6.2 %collective-permute-start.6 = (bf16[32,1,512]{2,0,1:T(8,128)(2,1)S(1)}, bf16[32,1,512]{2,0,1:T(8,128)(2,1)S(1)}, u32[]{:S(2)}, u32[]{:S(2)}) collective-permute-start(bf16[32,1,512]{2,0,1:T(8,128)(2,1)S(1)} %get-tuple-element.32), channel_id=1, source_target_pairs={{0,16},{16,32},{32,48},{48,64},{64,80},{80,96},{96,112},{1,17},{17... | collective-permute-start | bytes 98312 | tf_op jit(solution)/shard_map/ppermute | solution.py:17
  51.2 5.1 %collective-permute-start.7 = (bf16[32,1,512]{2,0,1:T(8,128)(2,1)S(1)}, bf16[32,1,512]{2,0,1:T(8,128)(2,1)S(1)}, u32[]{:S(2)}, u32[]{:S(2)}) collective-permute-start(bf16[32,1,512]{2,0,1:T(8,128)(2,1)S(1)} %get-tuple-element.33), channel_id=1, source_target_pairs={{16,0},{32,16},{48,32},{64,48},{80,64},{96,80},{112,96},{17,1},{33... | collective-permute-start | bytes 98312 | tf_op jit(solution)/shard_map/ppermute | solution.py:20
  62.0 7.8 %copy-start.1 = (bf16[256,3,3,512]{3,0,2,1:T(8,128)(2,1)S(1)}, bf16[256,3,3,512]{3,0,2,1:T(8,128)(2,1)}, u32[]{:S(2)}) copy-start(bf16[256,3,3,512]{3,0,2,1:T(8,128)(2,1)} %param.6) | copy-start | bytes 7077892
  62.0 74.4 %all-to-all-start = ((bf16[32,3,48,512]{3,0,1,2:T(8,128)(2,1)}), bf16[32,3,48,512]{3,0,1,2:T(8,128)(2,1)}, u32[]{:S(2)}, u32[]{:S(2)}) async-start(bf16[32,3,48,512]{3,0,1,2:T(8,128)(2,1)} %pad_maximum_fusion), calls=%async_computation | async-start | bytes 9437184 | tf_op jit(solution)/shard_map/all_to_all | solution.py:58
  69.6 258.8 %all-reduce.6.cloned.1.call-start = ((), (), s32[]{:S(2)}) async-start(), calls=%async_computation.2 | async-start | bytes 4718592 | tf_op jit(solution)/shard_map/psum | solution.py:95
  159.0 7.5 %copy-start = (bf16[512,4608]{1,0:T(8,128)(2,1)S(1)}, bf16[512,4608]{1,0:T(8,128)(2,1)}, u32[]{:S(2)}) copy-start(bf16[512,4608]{1,0:T(8,128)(2,1)} %reshape.23) | copy-start | bytes 14155780
  159.0 7.5 %copy-start.4 = (bf16[256,3,3,512]{0,3,2,1:T(8,128)(2,1)S(1)}, bf16[256,3,3,512]{0,3,2,1:T(8,128)(2,1)}, u32[]{:S(2)}) copy-start(bf16[256,3,3,512]{0,3,2,1:T(8,128)(2,1)} %copy.30) | copy-start | bytes 7077892
  179.8 152.7 %copy-start.7 = (bf16[768,512]{1,0:T(8,128)(2,1)S(1)}, bf16[768,512]{1,0:T(8,128)(2,1)}, u32[]{:S(2)}) copy-start(bf16[768,512]{1,0:T(8,128)(2,1)} %param.9) | copy-start | bytes 2359300
  328.4 4.1 copy-start.5
  355.0 95.5 %all-to-all-start.1 = ((bf16[512,3,3,512]{3,2,1,0:T(4,128)(2,1)}), bf16[512,3,3,512]{3,2,1,0:T(4,128)(2,1)}, u32[]{:S(2)}, u32[]{:S(2)}) async-start(bf16[512,3,3,512]{3,2,1,0:T(4,128)(2,1)} %copy.33), calls=%async_computation.1 | async-start | bytes 12582912 | tf_op jit(solution)/shard_map/all_to_all | solution.py:103
Sparse Core Ops, SparseCore 0:
  171.2 157.1 all-reduce.5
where the time goes:
time: 475 us; the launch traced here: 468 us
  waiting for transfers between devices  307 us (65%)
  local copies, waits for them, and re-layouts  47.9 us (10%)
  starting transfers between devices  37 us (8%)
  other arithmetic  30 us (6%)
  matrix products  29.3 us (6%)
  between operations  16.8 us (4%)
    psum x1, waiting for transfers between devices, shards(): gram_all = lax.psum(gram_local, ('space', 'mode')) / cell_count  149 us
    all_to_all x1, waiting for transfers between devices, shards(): lax.all_to_all(scaled_rows, 'mode', split_axis=0, concat_axis=2, tiled=True)  87 us
    all_to_all x1, waiting for transfers between devices, shards(): lax.all_to_all(prior_factors, 'mode', split_axis=2, concat_axis=0, tiled=...  62.6 us
    ppermute x4, starting transfers between devices, extended(): lax.ppermute(lax.slice_in_dim(block, block.shape[dim] - width, None, axis...  17.6 us
    reshape x1, local copies, waits for them, and re-layouts, shards(): prior_latitudes = rebanded_factors.reshape(factor_tally, -1)  13.5 us
    convert_element_type x1, local copies, waits for them, and re-layouts, shards(): (inflation * truncated_factors).reshape(rebanded_factors.shape)  11 us
  transfers between devices with their start and end apart: 11, of which 7 were waited for; matrix products, arithmetic and copies ran while one was open for 3% of the time, Pallas kernels for 0%

commit v1 on v0

v1 whole, which is shorter than its diff:
```python
import jax
import jax.numpy as jnp
from jax import lax
from jax.experimental import pallas as pl
from jax.experimental.pallas import tpu as pltpu
from jax.sharding import PartitionSpec as P

flux_coef = 0.2
slope_coef = 0.2
turn_coef = 0.1
keep_coef = 0.95

MESH = pl.DeviceIdType.MESH
F32, BF16 = jnp.float32, jnp.bfloat16
NM, NZ, NY, NX = 16, 4, 4, 4
ROWS, COLS, LOCAL, PAIRS = 48, 512, 32, 9
MODES, NOISE, WIDE = 512, 256, 768
BAND, PIECE = WIDE // 8, 6
CELLS = 3.0 * 384 * 512
OFFSETS = [
    (0, 1), (1, 0), (0, 3), (3, 0), (1, 1), (0, 2), (3, 3), (2, 0),
    (1, 3), (1, 2), (3, 1), (3, 2), (2, 1), (2, 2), (2, 3),
]


def kernel(
    x_in, depth_in, mask_in, noise_in, rot_in, out, gram_out, infl_out,
    X, D, M, DN, DA, DB, W, S1, E1, N1, S2, F, L, R, G, G0, H, G1, K, G2, T,
    C0, C0r, C1, C2, gram_pad,
    sem_x, sem_load, sem_own, sem_halo_s, sem_halo_r, sem_fs, sem_fr, sem_bs, sem_br,
    sem_g0s, sem_g0r, sem_g1s, sem_g1r, sem_g2s, sem_g2r, sem_cs, sem_cr,
):
    space, mode = lax.axis_index("space"), lax.axis_index("mode")
    z, c = space // 2, lax.rem(space, 2)
    y, x = mode // NX, lax.rem(mode, NX)

    def mode_of(offset):
        return lax.rem(y + offset[0], NY) * NX + lax.rem(x + offset[1], NX)

    up, down = lax.rem(space + 1, 8), lax.rem(space + 7, 8)
    partner = z * 2 + (1 - c)
    far = lax.rem(space + 7 + 2 * c, 8)

    def z_of(k):
        return lax.rem(z + k, NZ)

    def remote(src, dst, send, recv, s, m):
        return pltpu.make_async_remote_copy(
            src_ref=src, dst_ref=dst, send_sem=send, recv_sem=recv,
            device_id=(s, m), device_id_type=MESH,
        )

    load_x = pltpu.make_async_copy(x_in, X.at[pl.ds(4, ROWS)], sem_x.at[0])
    load_d = pltpu.make_async_copy(depth_in, D.at[pl.ds(8, ROWS)], sem_x.at[1])
    load_m = pltpu.make_async_copy(mask_in, M.at[pl.ds(8, ROWS)], sem_x.at[2])
    load_e = pltpu.make_async_copy(noise_in, L.at[:, pl.ds(MODES, NOISE)], sem_load.at[0])
    load_t = pltpu.make_async_copy(rot_in, T, sem_load.at[1])
    for copy in (load_d, load_m, load_x, load_e, load_t):
        copy.start()

    barrier = pltpu.get_barrier_semaphore()
    peers = [(space, mode_of(o)) for o in OFFSETS]
    peers += [(partner, mode), (far, mode)] + [(z_of(k) * 2 + c, mode) for k in (1, 2, 3)]
    for s, m in peers:
        pl.semaphore_signal(barrier, inc=1, device_id=(s, m), device_id_type=MESH)
    pl.semaphore_wait(barrier, len(peers))

    halos = [
        remote(x_in.at[pl.ds(44, 4)], X.at[pl.ds(0, 4)], sem_halo_s.at[0], sem_halo_r.at[0], up, mode),
        remote(x_in.at[pl.ds(0, 4)], X.at[pl.ds(52, 4)], sem_halo_s.at[1], sem_halo_r.at[1], down, mode),
        remote(depth_in.at[pl.ds(40, 8)], D.at[pl.ds(0, 8)], sem_halo_s.at[2], sem_halo_r.at[2], up, mode),
        remote(depth_in.at[pl.ds(0, 8)], D.at[pl.ds(56, 8)], sem_halo_s.at[3], sem_halo_r.at[3], down, mode),
        remote(mask_in.at[pl.ds(40, 8)], M.at[pl.ds(0, 8)], sem_halo_s.at[4], sem_halo_r.at[4], up, mode),
        remote(mask_in.at[pl.ds(0, 8)], M.at[pl.ds(56, 8)], sem_halo_s.at[5], sem_halo_r.at[5], down, mode),
    ]
    for copy in halos:
        copy.start()

    lane = lax.broadcasted_iota(jnp.int32, (1, COLS), 1)
    first, last = lane == 0, lane == COLS - 1

    def prepare(lo, count, inside):
        rows = pl.ds(lo, count)
        depth = jnp.where(inside, D[rows, :] * flux_coef, 0.0)
        DN[rows, :] = depth
        DA[rows, :] = jnp.where(first, 0.0, depth)
        DB[rows, :] = jnp.where(last, 0.0, depth)
        W[rows, :] = jnp.where(inside, M[rows, :].astype(F32), 0.0)

    load_d.wait()
    load_m.wait()
    prepare(8, ROWS, True)
    load_x.wait()

    def halves(row):
        for g in range(2):
            row(pl.ds(16 * g, 16))

    def surface(q, g, s, e, n):
        t = q + 4
        flow = e(q, g)
        across = pltpu.roll(DA[pl.ds(t, 1), :] * flow, COLS - 1, 1) - pltpu.roll(
            DB[pl.ds(t, 1), :] * flow, 1, 1
        )
        along = DN[pl.ds(t + 1, 1), :] * n(q + 1, g) - DN[pl.ds(t - 1, 1), :] * n(q - 1, g)
        return W[pl.ds(t, 1), :] * (s(q, g) - (across + along))

    def flows(q, g, s, e, n):
        wet = W[pl.ds(q + 4, 1), :]
        here, east, north = s(q, g), e(q, g), n(q, g)
        slope = pltpu.roll(jnp.where(first, 0.0, here), COLS - 1, 1) - pltpu.roll(
            jnp.where(last, 0.0, here), 1, 1
        )
        east_new = wet * (keep_coef * east + turn_coef * north - slope_coef * slope)
        slope = s(q + 1, g) - s(q - 1, g)
        north_new = wet * (keep_coef * north - turn_coef * east - slope_coef * slope)
        return east_new, north_new

    def raw(field):
        return lambda q, g: X[q, field, g, :].astype(F32)

    def held(ref):
        return lambda q, g: ref[q, g, :]

    raws, firsts = [raw(f) for f in range(3)], [held(r) for r in (S1, E1, N1)]

    def surface_1(q):
        def row(g):
            S1[q, g, :] = surface(q, g, *raws)

        halves(row)

    def flows_1(q):
        def row(g):
            E1[q, g, :], N1[q, g, :] = flows(q, g, held(S1), raws[1], raws[2])

        halves(row)

    pl.loop(5, 51)(surface_1)
    pl.loop(6, 50)(flows_1)
    for copy in halos:
        copy.wait()
    prepare(0, 8, space > 0)
    prepare(56, 8, space < 7)

    @pl.loop(0, 8)
    def _(i):
        surface_1(jnp.where(i < 4, i + 1, i + 47))

    @pl.loop(0, 8)
    def _(i):
        flows_1(jnp.where(i < 4, i + 2, i + 46))

    def surface_2(q):
        def row(g):
            S2[q, g, :] = surface(q, g, *firsts)

        halves(row)

    surface_2(3)
    surface_2(52)

    @pl.loop(0, NM)
    def _(m):
        for i in range(3):
            q = 3 * m + i + 4

            def row(g, i=i, q=q):
                value = surface(q, g, *firsts)
                S2[q, g, :] = value
                F[m, i, g, :] = value.astype(BF16)

            halves(row)

    def send_pair(r):
        for o in OFFSETS:
            m = mode_of(o)
            remote(
                F.at[m, r], L.at[r, pl.ds(pl.multiple_of(mode * LOCAL, LOCAL), LOCAL)],
                sem_fs, sem_fr.at[r], space, m,
            ).start()

    pl.loop(0, 3)(send_pair)

    @pl.loop(0, NM)
    def _(m):
        for i in range(3):
            q = 3 * m + i + 4

            def row(g, i=i, q=q):
                east, north = flows(q, g, held(S2), firsts[1], firsts[2])
                F[m, 3 + i, g, :] = east.astype(BF16)
                F[m, 6 + i, g, :] = north.astype(BF16)

            halves(row)

    pl.loop(3, PAIRS)(send_pair)
    own = pl.ds(pl.multiple_of(mode * LOCAL, LOCAL), LOCAL)
    own_in = pltpu.make_async_copy(F.at[mode], L.at[:, own], sem_own.at[0])
    own_in.start()
    load_e.wait()
    load_t.wait()
    G[...] = jnp.zeros_like(G)
    C0[...] = jnp.zeros_like(C0)
    own_in.wait()

    def folded(value):
        value = value * value
        value = jnp.sum(value.reshape(-1, 8, value.shape[-1]), axis=0)
        return sum(value[:, 128 * k : 128 * (k + 1)] for k in range(value.shape[-1] // 128))

    @pl.loop(0, PAIRS)
    def _(r):
        pltpu.make_async_copy(
            L.at[r, pl.ds(0, MODES - LOCAL)], L.at[r, pl.ds(0, MODES - LOCAL)], sem_fr.at[r]
        ).wait()
        for b in range(2):
            part = pl.ds(256 * b, 256)
            rotated = jnp.dot(T[part, :], L[r], preferred_element_type=F32)
            C0[1] += folded(rotated)
            R[r, part, :] = rotated.astype(BF16)
        for o in OFFSETS:
            m = mode_of(o)
            remote(
                R.at[r, pl.ds(pl.multiple_of(m * LOCAL, LOCAL), LOCAL)], out.at[mode, r],
                sem_bs, sem_br, space, m,
            ).start()
        for b in range(3):
            part = pl.ds(256 * b, 256)
            block = L[r, part, :]
            C0[0] += folded(block.astype(F32))
            G[part, :] += lax.dot_general(
                block, L[r], (((1,), (1,)), ((), ())), preferred_element_type=F32
            )

    own_out = pltpu.make_async_copy(R.at[:, own], out.at[mode], sem_own.at[1])
    own_out.start()

    send_c0 = remote(C0, C0r, sem_cs.at[0], sem_cr.at[0], partner, mode)
    send_c0.start()
    for k in range(NZ):
        remote(
            G.at[pl.ds(pl.multiple_of((2 * k + 1 - c) * BAND, 8), BAND)], G0.at[k],
            sem_g0s, sem_g0r, partner, mode,
        ).start()
    send_c0.wait()
    C1[z] = C0[...] + C0r[...]
    for k in (1, 2, 3):
        remote(C1.at[z], C1.at[z], sem_cs.at[1], sem_cr.at[1], z_of(k) * 2 + c, mode).start()
    wait_c1 = remote(C1.at[pl.ds(0, 3)], C1.at[pl.ds(0, 3)], sem_cs.at[1], sem_cr.at[1], partner, mode)
    wait_c1.wait()
    C2[mode] = ((C1[0] + C1[1]) + C1[2]) + C1[3]
    for o in OFFSETS:
        remote(C2.at[mode], C2.at[mode], sem_cs.at[2], sem_cr.at[2], space, mode_of(o)).start()

    remote(G0, G0, sem_g0s, sem_g0r, partner, mode).wait()

    @pl.loop(0, NZ)
    def _(k):
        for b in range(4):
            rows = pl.ds(24 * b, 24)
            mine = pl.ds(pl.multiple_of((2 * k + c) * BAND + 24 * b, 8), 24)
            H[k, rows, :] = G[mine, :] + G0[k, rows, :]

    for k in (1, 2, 3):
        remote(H.at[z_of(k)], G1.at[k - 1], sem_g1s, sem_g1r, z_of(k) * 2 + c, mode).start()
    remote(G1, G1, sem_g1s, sem_g1r, partner, mode).wait()
    for m in range(NM):
        rows = pl.ds(PIECE * m, PIECE)
        total = (H[z, rows, :] + G1[0, rows, :]) + (G1[1, rows, :] + G1[2, rows, :])
        K[m, pl.ds(0, PIECE), :] = total
        K[m, pl.ds(PIECE, 2), :] = jnp.zeros((2, WIDE), F32)
    for o in OFFSETS:
        m = mode_of(o)
        remote(K.at[m], G2.at[mode], sem_g2s, sem_g2r, space, m).start()
    G2[mode] = K[mode]

    many = pl.ds(0, NM - 1)
    remote(C2.at[many], C2.at[many], sem_cs.at[2], sem_cr.at[2], partner, mode).wait()
    total = C2[0]
    for m in range(1, NM):
        total = total + C2[m]
    full = jnp.sum(jnp.sum(total[0], axis=0, keepdims=True), axis=1, keepdims=True)
    kept = jnp.sum(jnp.sum(total[1], axis=0, keepdims=True), axis=1, keepdims=True)
    infl_out[...] = jnp.broadcast_to(jnp.sqrt(full / kept), infl_out.shape)

    remote(G2.at[many], G2.at[many], sem_g2s, sem_g2r, partner, mode).wait()
    gram_pad[...] = jnp.sum(G2[...], axis=0) / CELLS
    gram_out[...] = gram_pad[pl.ds(0, PIECE), :]

    own_out.wait()
    remote(F.at[many], F.at[many], sem_fs, sem_br, partner, mode).wait_send()
    remote(out.at[many], out.at[many], sem_bs, sem_br, partner, mode).wait()


def shards(sqrt_factors, model_error, water_depth, sea_mask, givens_transform):
    fields = jnp.transpose(sqrt_factors, (2, 1, 0, 3))
    noise = jnp.transpose(model_error, (1, 2, 0, 3)).reshape(PAIRS, NOISE, COLS)
    rotation = givens_transform.T
    vmem, dma = pltpu.VMEM, pltpu.SemaphoreType.DMA
    anywhere = pl.BlockSpec(memory_space=pl.ANY)
    inside = pl.BlockSpec(memory_space=pltpu.VMEM)
    received, gram_rows, inflation = pl.pallas_call(
        kernel,
        out_shape=(
            jax.ShapeDtypeStruct((NM, PAIRS, LOCAL, COLS), BF16),
            jax.ShapeDtypeStruct((PIECE, WIDE), F32),
            jax.ShapeDtypeStruct((1, 128), F32),
        ),
        in_specs=[anywhere] * 5,
        out_specs=(anywhere, inside, inside),
        scratch_shapes=[
            vmem((ROWS + 8, 3, LOCAL, COLS), BF16),
            vmem((64, COLS), F32),
            vmem((64, COLS), jnp.int32),
            *[vmem((64, COLS), F32)] * 4,
            *[vmem((ROWS + 8, LOCAL, COLS), F32)] * 4,
            vmem((NM, PAIRS, LOCAL, COLS), BF16),
            vmem((PAIRS, WIDE, COLS), BF16),
            vmem((PAIRS, MODES, COLS), BF16),
            vmem((WIDE, WIDE), F32),
            vmem((NZ, BAND, WIDE), F32),
            vmem((NZ, BAND, WIDE), F32),
            vmem((NZ - 1, BAND, WIDE), F32),
            vmem((NM, 8, WIDE), F32),
            vmem((NM, 8, WIDE), F32),
            vmem((MODES, WIDE), BF16),
            vmem((2, 8, 128), F32),
            vmem((2, 8, 128), F32),
            vmem((NZ, 2, 8, 128), F32),
            vmem((NM, 2, 8, 128), F32),
            vmem((8, WIDE), F32),
            dma((3,)), dma((2,)), dma((2,)), dma((6,)), dma((6,)),
            dma, dma((PAIRS,)), dma, dma,
            dma, dma, dma, dma, dma, dma, dma((3,)), dma((3,)),
        ],
        compiler_params=pltpu.CompilerParams(
            collective_id=0, has_side_effects=True, vmem_limit_bytes=60 << 20
        ),
    )(fields, water_depth, sea_mask, noise, rotation)
    inflation = inflation[0, 0]
    scaled = (inflation * received.astype(F32)).astype(BF16)
    scaled = scaled.reshape(NM, 3, 3, LOCAL, COLS)
    reduced = jnp.transpose(scaled, (3, 1, 0, 2, 4)).reshape(sqrt_factors.shape)
    return (reduced, gram_rows, inflation)


def solution(mesh):
    in_specs = (
        P("mode", None, "space", None),
        P(None, None, ("space", "mode"), None),
        P("space", None),
        P("space", None),
        P(),
    )
    out_specs = (P("mode", None, "space", None), P(("space", "mode"), None), P())
    return jax.shard_map(shards, mesh=mesh, in_specs=in_specs, out_specs=out_specs, check_vma=False)
```

time: 475 us -> 154 us (0.32); the launches traced: 468 us -> 153 us
  waiting for transfers between devices: 307 us -> 0 us
  Pallas kernels: 0 us -> 131 us
  starting transfers between devices: 37 us -> 0 us
  local copies, waits for them, and re-layouts: 47.9 us -> 15.6 us
  matrix products: 29.3 us -> 0 us
  other arithmetic: 30 us -> 4.07 us
  between operations: 16.8 us -> 1.84 us
    all_to_all x2 -> x0, waiting for transfers between devices: 150 us -> none  [the longest x1 87 us: shards(): lax.all_to_all(scaled_rows, 'mode', split_axis=0, concat_axis=2, tiled=True)]
    psum x1 -> x0, waiting for transfers between devices: 149 us -> none  [shards(): gram_all = lax.psum(gram_local, ('space', 'mode')) / cell_count]
    pallas_call x0 -> x1, Pallas kernels: none -> 131 us  [shards(): pl.pallas_call(kernel, out_shape=(jax.ShapeDtypeStruct((NM, PAIRS, LOCAL,...]
    dot_general x6 -> x0, matrix products: 29.3 us -> none  [the longest x1 8.74 us: shards(): lax.dot_general(givens_transform[:factor_tally], prior_latitudes, pairwis...]
    ppermute x8 -> x0, starting transfers between devices: 22.8 us -> none  [the longest x4 17.6 us: extended(): lax.ppermute(lax.slice_in_dim(block, block.shape[dim] - width, None, axis...]
    all_to_all x2 -> x0, starting transfers between devices: 14 us -> none  [the longest x1 7.61 us: shards(): lax.all_to_all(prior_factors, 'mode', split_axis=2, concat_axis=0, tiled=...]
    all_to_all x3 -> x0, local copies, waits for them, and re-layouts: 13.8 us -> none  [the longest x1 9.15 us: shards(): lax.all_to_all(prior_factors, 'mode', split_axis=2, concat_axis=0, tiled=...]
    reshape x1, local copies, waits for them, and re-layouts: 13.5 us -> 0.71 us  [shards(): scaled = scaled.reshape(NM, 3, 3, LOCAL, COLS)]
  transfers between devices with their start and end apart: 11 -> 0, of which waited for: 7 -> 0; matrix products, arithmetic and copies ran while one was open for 3% -> 0% of each run, Pallas kernels for 0% -> 0%
where the time goes in v1:
time: 154 us; the launch traced here: 153 us
  Pallas kernels  131 us (85%)
  local copies, waits for them, and re-layouts  15.6 us (10%)
  other arithmetic  4.07 us (3%)
  between operations  1.84 us (1%)
    pallas_call x1, Pallas kernels, shards(): pl.pallas_call(kernel, out_shape=(jax.ShapeDtypeStruct((NM, PAIRS, LOCAL,...  131 us
    unnamed x8, local copies, waits for them, and re-layouts  14.9 us
    convert_element_type x1, other arithmetic, shards(): scaled = (inflation * received.astype(F32)).astype(BF16)  4.07 us

profile of v1, /device:TPU:2, one launch (start us, length us, event | category | flops | bytes accessed | tf_op | source)
XLA Modules:
  0.0 152.8 jit_solution(7466583043797362584)
XLA Ops:
  0.6 2.3 %copy.12 = bf16[768,512]{0,1:T(8,128)(2,1)} copy(bf16[768,512]{1,0:T(8,128)(2,1)} %param.9) | data formatting | bytes 1572864 | tf_op args[4]
  2.9 7.2 %copy.16 = bf16[32,3,48,512]{3,0,1,2:T(8,128)(2,1)} copy(bf16[32,3,48,512]{3,2,1,0:T(8,128)(2,1)} %param.5) | data formatting | bytes 9437184 | tf_op args[0]
  10.1 131.3 %shard_map.76 = (bf16[16,9,32,512]{3,2,1,0:T(8,128)(2,1)}, f32[6,768]{1,0:T(8,128)}, f32[1,128]{1,0:T(1,128)}) custom-call(bf16[48,3,32,512]{3,2,1,0:T(8,128)(2,1)} %bitcast.15, f32[48,512]{1,0:T(8,128)} %depth_in.1, s32[48,512]{1,0:T(8,128)} %mask_in.1, bf16[9,256,512]{2,1,0:T(8,128)(2,1)} %bitcast.17, bf16[512,768]{1,0:T(8,128)(2,1)} %bitcast.16), custom_call_target="tpu_custom_call" | custom-call | tf_op jit(solution)/shard_map/pallas_call | solution.py:303
  141.3 4.1 %multiply_convert_fusion = bf16[16,9,32,512]{3,2,1,0:T(8,128)(2,1)S(1)} fusion(bf16[16,9,32,512]{3,2,1,0:T(8,128)(2,1)} %get-tuple-element.7, f32[]{:T(128)} %bitcast.18), kind=kLoop, calls=%fused_computation | loop fusion | flops 7077888 | bytes 9437188 | tf_op jit(solution)/shard_map/convert_element_type | solution.py:342
  145.4 0.7 copy.13
  146.1 0.0 copy-start
  146.2 0.0 copy-start.1
  146.2 4.9 %copy.14 = bf16[32,3,48,512]{3,2,1,0:T(8,128)(2,1)} copy(bf16[32,3,48,512]{3,0,2,1:T(8,128)(2,1)S(1)} %bitcast.14) | data formatting | bytes 9437184
  151.0 0.0 copy-done
  151.0 0.6 copy.19
  151.6 0.0 copy-done.1
Async XLA Ops:
  146.1 4.9 %copy-start = (f32[6,768]{1,0:T(8,128)S(1)}, f32[6,768]{1,0:T(8,128)}, u32[]{:S(2)}) copy-start(f32[6,768]{1,0:T(8,128)} %get-tuple-element.16) | copy-start | bytes 55300
  146.2 5.5 %copy-start.1 = (f32[1,128]{1,0:T(1,128)S(1)}, f32[1,128]{1,0:T(1,128)}, u32[]{:S(2)}) copy-start(f32[1,128]{1,0:T(1,128)} %get-tuple-element.6) | copy-start | bytes 1540
